TPU v7x, 32 devices: a whole 2x2x4 slice. The times are simulated.
32 devices in a mesh: row: 8 (over y, x, core), col: 4 (over z).
Axes of the slice: x: 2, y: 2, z: 4, core: 2. Of those that a mesh axis runs over, the one named last changes fastest.
Arguments:
- k_blocks: bfloat16 [24, 16, 64, 64], P('row', 'col'), may hold values from -0.25 to 0.25
- p_blocks: bfloat16 [24, 16, 64, 128], P('row', 'col'), may hold values from -6 to 6
- k_columns: int32 [24, 16], P('row', 'col'), may hold values from -1 to 23, as said below
- p_columns: int32 [24, 16], P('row', 'col'), may hold values from -1 to 23, as said below
- molecule_order: int32 [24], replicated, may hold values from 0 to 23, as said below
Outputs:
- commutator: bfloat16 [24, 16, 64, 128], P('row', 'col')
Inputs may be any that keep to these rules, and one draw needn't show every extreme that they name: `molecule_order`: a permutation of 0 to 23. `k_columns`: -1 marks an empty slot; the live slots 4 * g to 4 * g + 3 of a block row hold molecules whose stored block index lies in [g * 6, (g + 1) * 6); live entries of one block row are distinct; every slot of the group holding a row's own stored index is live. `p_columns`: the same rules as for k_columns, with another pattern.
All inputs are finite; a program needn't handle non-finite values.
Results may differ from a plain program's by a relative error of at most 0.001.
Values may be sent and summed in bfloat16 or wider, within the bound.
A program may use at most 128 MiB of HBM per device.

v0:
```python
import jax
import jax.numpy as jnp
from jax import lax
from jax.sharding import PartitionSpec as P


def storage_of(columns, molecule_order):
    agrees = columns[..., None] == molecule_order
    position = jnp.sum(
        jnp.where(agrees, jnp.arange(molecule_order.shape[0], dtype=jnp.int32), 0), axis=-1
    )
    return jnp.where(columns >= 0, position, -1)


def select_blocks(wanted, out_columns, group_vals, group_columns, first_row, span_rows):
    offset = wanted - first_row
    inside = (wanted >= 0) & (offset >= 0) & (offset < span_rows)
    row_pick = jnp.clip(offset, 0, span_rows - 1).astype(jnp.int32)
    slot_width = group_columns.shape[1]
    row_columns = group_columns[row_pick]
    agrees = (row_columns[..., :, None] == out_columns[:, None, None, :]) & (
        row_columns[..., :, None] >= 0
    )
    slot_pick = jnp.sum(
        jnp.where(agrees, jnp.arange(slot_width, dtype=jnp.int32)[:, None], 0), axis=-2
    )
    matched = jnp.any(agrees, axis=-2) & inside[..., None]
    flattened = group_vals.reshape((span_rows * slot_width,) + group_vals.shape[2:])
    picked = flattened[row_pick[..., None] * slot_width + slot_pick]
    return jnp.where(matched[..., None, None], picked, jnp.zeros((), picked.dtype))


def product_left(k_piece, p_chosen):
    return jnp.einsum("isxy,istyz->itxz", k_piece, p_chosen, preferred_element_type=jnp.float32)


def product_right(p_piece, k_chosen):
    row_total, slot_total, block_edge, double_edge = p_piece.shape
    halves = p_piece.reshape(row_total, slot_total, block_edge, 2, double_edge // 2)
    result = jnp.einsum("isxcy,istyz->itxcz", halves, k_chosen, preferred_element_type=jnp.float32)
    return result.reshape(row_total, result.shape[1], block_edge, double_edge)


def per_device(k_blocks, p_blocks, k_columns, p_columns, molecule_order):
    k_cols = storage_of(k_columns, molecule_order)
    p_cols = storage_of(p_columns, molecule_order)
    p_group, p_group_cols, k_group, k_group_cols = (
        lax.all_gather(p_blocks, "row", axis=0, tiled=True),
        lax.all_gather(p_cols, "row", axis=0, tiled=True),
        lax.all_gather(k_blocks, "row", axis=0, tiled=True),
        lax.all_gather(k_cols, "row", axis=0, tiled=True),
    )
    group_rows = p_group.shape[0]
    pieces = (
        lax.all_gather(k_blocks, "col", axis=1, tiled=True),
        lax.all_gather(k_cols, "col", axis=1, tiled=True),
    )
    p_chosen = select_blocks(pieces[1], p_cols, p_group, p_group_cols, 0, group_rows)
    k_then_p = product_left(pieces[0], p_chosen)
    pieces = (
        lax.all_gather(p_blocks, "col", axis=1, tiled=True),
        lax.all_gather(p_cols, "col", axis=1, tiled=True),
    )
    k_chosen = select_blocks(pieces[1], p_cols, k_group, k_group_cols, 0, group_rows)
    p_then_k = product_right(pieces[0], k_chosen)
    combined = k_then_p - p_then_k
    return combined.astype(jnp.bfloat16)


def solution(mesh):
    in_specs = (
        P("row", "col", None, None),
        P("row", "col", None, None),
        P("row", "col"),
        P("row", "col"),
        P(),
    )
    out_specs = P("row", "col", None, None)
    return jax.shard_map(
        per_device, mesh=mesh, in_specs=in_specs, out_specs=out_specs, check_vma=False
    )
```

profile of v0, /device:TPU:0, one launch (start us, length us, event | category | flops | bytes accessed | tf_op | source)
XLA Modules:
  0.0 125.9 jit_solution(3691294378126330968)
XLA Ops:
  6.5 0.0 copy-start
  6.5 0.0 all-gather.6.cloned.1.call-start
  6.5 0.7 all-gather.6.cloned.1.call-update
  7.3 1.0 select_reduce_fusion.3
  8.2 0.7 fusion.19
  8.9 0.1 copy.72
  9.0 13.5 %all-gather.1 = s32[4,4,3]{2,1,0:T(4,128)S(1)} all-gather(s32[1,4,3]{2,1,0:T(4,128)S(1)} %bitcast.89), channel_id=1, replica_groups=mesh['row'=8,'col'=4] {'col'}, dimensions={0}, use_global_device_ids=true | all-gather | bytes 240 | tf_op jit(solution)/shard_map/all_gather | solution.py:56
  22.5 0.1 copy.73
  22.7 0.1 reshape.122
  22.8 0.1 reshape.76
  22.9 0.7 compare_select_fusion.5
  23.5 8.9 %all-gather = s32[8,3,4]{2,1,0:T(4,128)S(1)} all-gather(s32[1,3,4]{2,1,0:T(4,128)S(1)} %bitcast.87), channel_id=1, replica_groups=mesh['row'=8,'col'=4] {'row'}, dimensions={0}, use_global_device_ids=true | all-gather | bytes 432 | tf_op jit(solution)/shard_map/all_gather | solution.py:49
  32.4 0.6 gather_fusion
  33.0 0.1 copy.83
  33.1 11.9 %all-gather.3 = s32[4,4,3]{2,1,0:T(4,128)S(1)} all-gather(s32[1,4,3]{2,1,0:T(4,128)S(1)} %bitcast.90), channel_id=1, replica_groups=mesh['row'=8,'col'=4] {'col'}, dimensions={0}, use_global_device_ids=true | all-gather | bytes 240 | tf_op jit(solution)/shard_map/all_gather | solution.py:62
  45.0 0.1 copy.84
  45.1 0.1 reshape.129
  45.2 0.1 reshape.92
  45.3 8.9 %all-gather.2 = s32[8,3,4]{2,1,0:T(4,128)S(1)} all-gather(s32[1,3,4]{2,1,0:T(4,128)S(1)} %get-tuple-element.11), channel_id=1, replica_groups=mesh['row'=8,'col'=4] {'row'}, dimensions={0}, use_global_device_ids=true | all-gather | bytes 432 | tf_op jit(solution)/shard_map/all_gather | solution.py:51
  54.2 0.6 gather_fusion.2
  54.8 0.1 copy.75
  54.9 0.1 copy.86
  55.0 0.1 copy.76
  55.1 0.1 copy.87
  55.2 0.1 select_reduce_fusion.1
  55.3 0.1 copy.91
  55.4 0.1 reshape.100
  55.5 0.1 reshape.137
  55.6 0.1 fusion.17
  55.7 0.1 copy.90
  55.8 17.9 %all_gather.31 = bf16[3,16,64,128]{3,2,1,0:T(8,128)(2,1)S(1)} all-gather(bf16[3,4,64,128]{3,2,1,0:T(8,128)(2,1)} %param.6), channel_id=1, replica_groups=mesh['row'=8,'col'=4] {'col'}, dimensions={1}, use_global_device_ids=true | all-gather | bytes 983040 | tf_op jit(solution)/shard_map/all_gather | solution.py:61
  73.8 0.7 reshape.72
  74.5 0.0 copy-done
  74.5 12.2 %all_gather.30 = bf16[24,4,64,64]{3,2,1,0:T(8,128)(2,1)S(1)} all-gather(bf16[3,4,64,64]{3,2,1,0:T(8,128)(2,1)S(1)} %copy-done), channel_id=1, replica_groups=mesh['row'=8,'col'=4] {'row'}, dimensions={0}, use_global_device_ids=true | all-gather | bytes 884736 | tf_op jit(solution)/shard_map/all_gather | solution.py:50
  86.7 2.7 %gather_fusion.3 = bf16[192,64,64]{2,1,0:T(8,128)(2,1)} fusion(bf16[96,64,64]{2,1,0:T(8,128)(2,1)S(1)} %bitcast.77, s32[1024]{0:T(1024)S(1)} %pad_clamp_fusion), kind=kCustom, calls=%fused_computation.3 | custom fusion | bytes 3146496 | tf_op jit(solution)/shard_map/gather | solution.py:29
  89.4 4.3 %fusion = f32[3,4,64,64,2,1]{3,2,5,4,1,0:T(8,128)S(1)} fusion(bf16[3,16,64,2,64,1]{4,3,2,1,0,5:T(2,128)(2,1)S(1)} %bitcast.81, bf16[3,16,4,64,64]{4,3,2,1,0:T(8,128)(2,1)} %bitcast.80, pred[3,16,4]{2,1,0:T(8,128)(4,1)S(1)} %copy.90), kind=kOutput, calls=%fused_computation.4 | convolution fusion | flops 202113024 | bytes 2752704 | tf_op jit(solution)/shard_map/isxcy,istyz->itxcz/dot_general | solution.py:40
  93.8 1.0 copy.106
  94.8 0.1 copy.80
  94.9 0.1 reshape.84
  95.0 0.1 reshape.136
  95.1 0.1 copy.79
  95.2 18.7 %all_gather.27 = bf16[3,16,64,64]{3,2,1,0:T(8,128)(2,1)} all-gather(bf16[3,4,64,64]{3,2,1,0:T(8,128)(2,1)S(1)} %copy-done), channel_id=1, replica_groups=mesh['row'=8,'col'=4] {'col'}, dimensions={1}, use_global_device_ids=true | all-gather | bytes 491520 | tf_op jit(solution)/shard_map/all_gather | solution.py:55
  113.9 0.0 all-gather.6.cloned.1.call-done
  113.9 0.0 copy-start.1
  113.9 2.6 %gather_fusion.1 = bf16[192,64,128]{2,1,0:T(8,128)(2,1)S(1)} fusion(bf16[96,64,128]{2,1,0:T(8,128)(2,1)} %bitcast.78, s32[1024]{0:T(1024)S(1)} %pad_clamp_fusion.2), kind=kCustom, calls=%fused_computation.1 | custom fusion | bytes 6292224 | tf_op jit(solution)/shard_map/gather | solution.py:29
  116.5 0.0 copy-done.1
  116.6 2.5 %fusion.13 = bf16[3,4,64,128]{3,2,1,0:T(8,128)(2,1)} fusion(f32[3,4,64,128]{3,2,1,0:T(8,128)S(1)} %copy-done.1, bf16[3,16,4,64,128]{4,3,2,1,0:T(8,128)(2,1)S(1)} %bitcast.79, pred[3,16,4]{2,1,0:T(8,128)(4,1)S(1)} %copy.79, bf16[3,16,64,64]{3,2,1,0:T(8,128)(2,1)} %all_gather.27), kind=kOutput, calls=%fused_computation.14 | convolution fusion | flops 203096064 | bytes 4128960 | tf_op jit(solution)/shard_map/isxy,istyz->itxz/dot_general | solution.py:34
  (17 shorter events, 0.1 us)
Async XLA Ops:
  6.5 68.0 %copy-start = (bf16[3,4,64,64]{3,2,1,0:T(8,128)(2,1)S(1)}, bf16[3,4,64,64]{3,2,1,0:T(8,128)(2,1)}, u32[]{:S(2)}) copy-start(bf16[3,4,64,64]{3,2,1,0:T(8,128)(2,1)} %param.5) | copy-start | bytes 294916
  6.5 107.4 %all-gather.6.cloned.1.call-start = ((), (), s32[]{:S(2)}) async-start(), calls=%async_computation | async-start | bytes 1769472 | tf_op jit(solution)/shard_map/all_gather | solution.py:48
  113.9 2.6 %copy-start.1 = (f32[3,4,64,128]{3,2,1,0:T(8,128)S(1)}, f32[3,4,64,128]{3,2,1,0:T(8,128)}, u32[]{:S(2)}) copy-start(f32[3,4,64,128]{3,2,1,0:T(8,128)} %copy.106) | copy-start | bytes 1179652
Sparse Core Ops, SparseCore 0:
  9.2 28.3 all-gather.5
where the time goes:
time: 126 us
  blocking collectives  92 us (73%)
  between operations  13.5 us (11%)
  local copies, waits for them, and re-layouts  10.2 us (8%)
  matrix products  6.89 us (5%)
  other arithmetic  2.67 us (2%)
    all_gather x1, blocking collectives, per_device(): lax.all_gather(k_blocks, 'col', axis=1, tiled=True)  18.7 us
    all_gather x1, blocking collectives, per_device(): lax.all_gather(p_blocks, 'col', axis=1, tiled=True)  17.9 us
    all_gather x1, blocking collectives, per_device(): lax.all_gather(k_cols, 'col', axis=1, tiled=True)  13.5 us
    all_gather x1, blocking collectives, per_device(): lax.all_gather(k_blocks, 'row', axis=0, tiled=True)  12.2 us
    all_gather x1, blocking collectives, per_device(): lax.all_gather(p_cols, 'col', axis=1, tiled=True)  11.9 us
    all_gather x1, blocking collectives, per_device(): lax.all_gather(p_cols, 'row', axis=0, tiled=True)  8.89 us
    all_gather x1, blocking collectives, per_device(): lax.all_gather(k_cols, 'row', axis=0, tiled=True)  8.87 us
    gather x2, local copies, waits for them, and re-layouts, select_blocks(): picked = flattened[row_pick[..., None] * slot_width + slot_pick]  5.34 us
  transfers between devices with their start and end apart: 1, of which 0 were waited for; matrix products, arithmetic and copies ran while one was open for 12% of the time, Pallas kernels for 0%

commit v1 on v0

v1 whole, which is shorter than its diff:
```python
import functools

import jax
import jax.numpy as jnp
from jax import lax
from jax.experimental import pallas as pl
from jax.experimental.pallas import tpu as pltpu
from jax.sharding import PartitionSpec as P

MESH = pl.DeviceIdType.MESH
LANES = 128
TAB = 8


def swap_halves(x):
    half = x.shape[-1] // 2
    return pltpu.roll(x.astype(jnp.float32), half, x.ndim - 1).astype(x.dtype)


def kernel(
    nrow, ncol, R, S, G,
    kc_ref, pc_ref, order_ref, k_ref, p_ref, p_any, out_ref,
    pbuf, kbuf, kcol, plcol, mrow, mcol, mrow_s, mcol_s, jout, accl, accr,
    bar_unused, s_rp, r_rp, s_rk, r_rk, s_rm, r_rm, s_ck, r_ck, s_cp, r_cp, s_cm, r_cm, lsem,
):
    r = lax.axis_index("row")
    c = lax.axis_index("col")
    H = S // 2
    PB = R * S
    KB = R * H
    SW = nrow * KB
    zero_p = nrow * PB
    zero_k = 2 * SW
    B = k_ref.shape[2]

    rows = [lax.rem(r + d, nrow) for d in range(1, nrow)]
    cols = [lax.rem(c + d, ncol) for d in range(1, ncol)]

    barrier = pltpu.get_barrier_semaphore()
    for peer in rows:
        pl.semaphore_signal(barrier, inc=1, device_id={"row": peer}, device_id_type=MESH)
    for peer in cols:
        pl.semaphore_signal(barrier, inc=1, device_id={"col": peer}, device_id_type=MESH)

    lane = lax.broadcasted_iota(jnp.int32, (1, LANES), 1)
    meta = jnp.zeros((1, LANES), jnp.int32)
    entries = []
    orders = [order_ref[c * G + j] for j in range(G)]
    krow, kcl, prow, pcl = [], [], [], []
    t_p, t_kl, t_kh = [], [], []
    for i in range(R):
        kcs = [kc_ref[i, s] for s in range(S)]
        pcs = [pc_ref[i, s] for s in range(S)]
        khit = [[kcs[s] == orders[j] for j in range(G)] for s in range(S)]
        phit = [[pcs[s] == orders[j] for j in range(G)] for s in range(S)]
        for s in range(S):
            for hit, a, b, out in ((khit, krow, kcl, False), (phit, prow, pcl, True)):
                pos_r = jnp.int32(nrow)
                pos_c = jnp.int32(0)
                col = jnp.int32(G)
                for j in range(G):
                    q = c * G + j
                    pos_r = jnp.where(hit[s][j], q // R, pos_r)
                    pos_c = jnp.where(hit[s][j], lax.rem(q, R) * TAB, pos_c)
                    col = jnp.where(hit[s][j], j, col)
                a.append(pos_r)
                b.append(pos_c)
                if out:
                    jout[i * S + s] = col
        for j in range(TAB):
            vp, vl, vh = jnp.int32(zero_p), jnp.int32(zero_k), jnp.int32(zero_k)
            if j < G:
                for s in range(S):
                    pair = (r * R + i) * H + s // 2
                    vp = jnp.where(phit[s][j], (r * R + i) * S + s, vp)
                    vl = jnp.where(khit[s][j], pair + (s % 2) * SW, vl)
                    vh = jnp.where(khit[s][j], pair + (1 - s % 2) * SW, vh)
            t_p.append(vp)
            t_kl.append(vl)
            t_kh.append(vh)
    entries = t_p + t_kl + t_kh + krow + kcl + prow + pcl
    for n, v in enumerate(entries):
        meta = jnp.where(lane == n, v, meta)
    O_KL, O_KH = R * TAB, 2 * R * TAB
    O_KR = 3 * R * TAB
    O_KC, O_PR, O_PC = O_KR + PB, O_KR + 2 * PB, O_KR + 3 * PB
    mrow[r] = meta
    mcol[c] = meta
    empty = jnp.where(lane < O_KL, zero_p, zero_k)
    mrow[nrow] = empty

    low = lax.broadcasted_iota(jnp.int32, (B, 2 * B), 1) < B
    for i in range(R):
        for h in range(H):
            pair = jnp.concatenate([k_ref[i, 2 * h], k_ref[i, 2 * h + 1]], axis=-1)
            kbuf[r * KB + i * H + h] = pair
            kcol[c, i * H + h] = pair
            a, b = p_ref[i, 2 * h], p_ref[i, 2 * h + 1]
            plcol[c, i * H + h, :B] = jnp.where(low, a, swap_halves(b))
            plcol[c, i * H + h, B:] = jnp.where(low, swap_halves(a), b)

    pl.semaphore_wait(barrier, nrow + ncol - 2)

    def row_copies(src, d, peer):
        return (
            pltpu.make_async_remote_copy(
                mrow.at[src], mrow.at[src], s_rm.at[d], r_rm.at[src],
                device_id={"row": peer}, device_id_type=MESH),
            pltpu.make_async_remote_copy(
                kbuf.at[pl.ds(src * KB, KB)], kbuf.at[pl.ds(src * KB, KB)], s_rk.at[d], r_rk.at[src],
                device_id={"row": peer}, device_id_type=MESH),
            pltpu.make_async_remote_copy(
                p_any, pbuf.at[pl.ds(src * PB, PB)], s_rp.at[d], r_rp.at[src],
                device_id={"row": peer}, device_id_type=MESH),
        )

    def col_copies(src, d, peer):
        return (
            pltpu.make_async_remote_copy(
                mcol.at[src], mcol.at[src], s_cm.at[d], r_cm.at[src],
                device_id={"col": peer}, device_id_type=MESH),
            pltpu.make_async_remote_copy(
                kcol.at[src], kcol.at[src], s_ck.at[d], r_ck.at[src],
                device_id={"col": peer}, device_id_type=MESH),
            pltpu.make_async_remote_copy(
                plcol.at[src], plcol.at[src], s_cp.at[d], r_cp.at[src],
                device_id={"col": peer}, device_id_type=MESH),
        )

    sent = [row_copies(r, d, peer) for d, peer in enumerate(rows)]
    sent_col = [col_copies(c, d, peer) for d, peer in enumerate(cols)]
    for kind in range(3):
        for cp in sent_col:
            cp[kind].start()
        for cp in sent:
            cp[kind].start()

    for i in range(R):
        for s in range(S):
            pbuf[r * PB + i * S + s] = p_ref[i, s]
    zero = jnp.zeros((B, 2 * B), jnp.bfloat16)
    pbuf[zero_p] = zero
    kbuf[zero_k] = zero
    for n in range(KB):
        kbuf[SW + r * KB + n] = swap_halves(kbuf[r * KB + n])

    for d, src in enumerate(rows):
        row_copies(src, d, src)[0].wait_recv()
    for d, src in enumerate(cols):
        col_copies(src, d, src)[0].wait_recv()
    one = pltpu.make_async_copy(mrow, mrow_s, lsem.at[0])
    two = pltpu.make_async_copy(mcol, mcol_s, lsem.at[1])
    one.start()
    two.start()
    one.wait()
    two.wait()

    for d, src in enumerate(rows):
        row_copies(src, d, src)[1].wait_recv()
        for n in range(KB):
            kbuf[SW + src * KB + n] = swap_halves(kbuf[src * KB + n])
    for d, src in enumerate(rows):
        row_copies(src, d, src)[2].wait_recv()

    def add(g, first):
        for i in range(R):
            outs = [jout[i * S + t] for t in range(S)]
            right, right_k = [], []
            for s in range(S):
                qr, qc = mcol_s[g, 0, O_KR + i * S + s], mcol_s[g, 0, O_KC + i * S + s]
                right.append(jnp.concatenate(
                    [pbuf[mrow_s[qr, 0, qc + outs[t]]] for t in range(S)], axis=1))
                qr, qc = mcol_s[g, 0, O_PR + i * S + s], mcol_s[g, 0, O_PC + i * S + s]
                right_k.append(jnp.concatenate([
                    jnp.where(low,
                              kbuf[mrow_s[qr, 0, qc + outs[2 * h] + O_KL]],
                              kbuf[mrow_s[qr, 0, qc + outs[2 * h + 1] + O_KH]])
                    for h in range(H)], axis=1))
            left = jnp.concatenate([kcol[g, i * H + h] for h in range(H)], axis=1)
            kp = jnp.dot(left, jnp.concatenate(right, axis=0), preferred_element_type=jnp.float32)
            left = jnp.concatenate([plcol[g, i * H + h] for h in range(H)], axis=1)
            pk = jnp.dot(left, jnp.concatenate(right_k, axis=0), preferred_element_type=jnp.float32)
            if first:
                accl[i] = kp
                accr[i] = pk
            else:
                accl[i] += kp
                accr[i] += pk

    add(c, True)

    def step(d, carry):
        src = lax.rem(c + d, ncol)
        for cp in col_copies(src, 0, src)[1:]:
            cp.wait_recv()
        add(src, False)
        return carry

    lax.fori_loop(1, ncol, step, 0)

    for i in range(R):
        for h in range(H):
            re = accr[i, :B, h * 2 * B:(h + 1) * 2 * B]
            im = accr[i, B:, h * 2 * B:(h + 1) * 2 * B]
            first = jnp.where(low, re, pltpu.roll(im, B, 1))
            second = jnp.where(low, pltpu.roll(re, B, 1), im)
            for t, pk in ((2 * h, first), (2 * h + 1, second)):
                out_ref[i, t] = (accl[i, :, t * 2 * B:(t + 1) * 2 * B] - pk).astype(out_ref.dtype)

    for cps in sent + sent_col:
        for cp in cps:
            cp.wait_send()


def per_device(nrow, ncol, k_blocks, p_blocks, k_columns, p_columns, molecule_order):
    R, S, B, W = p_blocks.shape
    G = molecule_order.shape[0] // ncol
    H = S // 2
    bf, i32 = jnp.bfloat16, jnp.int32
    vmem = pl.BlockSpec(memory_space=pltpu.VMEM)
    smem = pl.BlockSpec(memory_space=pltpu.SMEM)
    dma = pltpu.SemaphoreType.DMA
    return pl.pallas_call(
        functools.partial(kernel, nrow, ncol, R, S, G),
        out_shape=jax.ShapeDtypeStruct(p_blocks.shape, bf),
        in_specs=[smem, smem, smem, vmem, vmem, pl.BlockSpec(memory_space=pl.ANY)],
        out_specs=vmem,
        scratch_shapes=[
            pltpu.VMEM((nrow * R * S + 1, B, W), bf),
            pltpu.VMEM((2 * nrow * R * H + 1, B, W), bf),
            pltpu.VMEM((ncol, R * H, B, W), bf),
            pltpu.VMEM((ncol, R * H, 2 * B, W), bf),
            pltpu.VMEM((nrow + 1, 1, LANES), i32),
            pltpu.VMEM((ncol, 1, LANES), i32),
            pltpu.SMEM((nrow + 1, 1, LANES), i32),
            pltpu.SMEM((ncol, 1, LANES), i32),
            pltpu.SMEM((R * S,), i32),
            pltpu.VMEM((R, B, S * W), jnp.float32),
            pltpu.VMEM((R, 2 * B, S * B), jnp.float32),
            dma((1,)),
            dma((nrow,)), dma((nrow,)), dma((nrow,)), dma((nrow,)), dma((nrow,)), dma((nrow,)),
            dma((ncol,)), dma((ncol,)), dma((ncol,)), dma((ncol,)), dma((ncol,)), dma((ncol,)),
            dma((2,)),
        ],
        compiler_params=pltpu.CompilerParams(
            collective_id=0, has_side_effects=True, vmem_limit_bytes=48 << 20),
    )(k_columns, p_columns, molecule_order, k_blocks,
      p_blocks, p_blocks.reshape(R * S, B, W))


def solution(mesh):
    in_specs = (
        P("row", "col", None, None),
        P("row", "col", None, None),
        P("row", "col"),
        P("row", "col"),
        P(),
    )
    out_specs = P("row", "col", None, None)
    body = functools.partial(per_device, mesh.shape["row"], mesh.shape["col"])
    return jax.shard_map(
        body, mesh=mesh, in_specs=in_specs, out_specs=out_specs, check_vma=False
    )
```

time: 126 us -> 39.9 us (0.32)
  the two profiles are of different devices: /device:TPU:0 before, /device:TPU:1 now
where the time goes in v1:
time: 39.9 us; the launch traced here: 39.7 us
  Pallas kernels  35.2 us (88%)
  local copies, waits for them, and re-layouts  4.55 us (11%)
    pallas_call x1, Pallas kernels, per_device(): pl.pallas_call(functools.partial(kernel, nrow, ncol, R, S, G), out_shape=...  35.2 us
    unnamed x11, local copies, waits for them, and re-layouts  4.55 us

profile of v1, /device:TPU:1, one launch (start us, length us, event | category | flops | bytes accessed | tf_op | source)
XLA Modules:
  0.0 39.7 jit_solution(17285145525682446372)
XLA Ops:
  0.0 0.0 copy-start.4
  0.0 0.7 %copy-done.4 = s32[24]{0:T(128)S(1)} copy-done((s32[24]{0:T(128)S(1)}, s32[24]{0:T(128)}, u32[]{:S(2)}) %copy-start.4) | copy-done | bytes 120
  0.7 0.0 copy-start
  0.7 0.9 %copy-done = bf16[3,4,64,128]{3,2,1,0:T(8,128)(2,1)S(1)} copy-done((bf16[3,4,64,128]{3,2,1,0:T(8,128)(2,1)S(1)}, bf16[3,4,64,128]{3,2,1,0:T(8,128)(2,1)}, u32[]{:S(2)}) %copy-start) | copy-done | bytes 196632
  1.6 0.0 copy-start.1
  1.6 0.9 %copy-done.1 = bf16[3,4,64,64]{3,2,1,0:T(8,128)(2,1)S(1)} copy-done((bf16[3,4,64,64]{3,2,1,0:T(8,128)(2,1)S(1)}, bf16[3,4,64,64]{3,2,1,0:T(8,128)(2,1)}, u32[]{:S(2)}) %copy-start.1) | copy-done | bytes 98328
  2.5 0.0 copy-start.2
  2.5 0.7 %copy-done.2 = s32[3,4]{1,0:T(4,128)S(1)} copy-done((s32[3,4]{1,0:T(4,128)S(1)}, s32[3,4]{1,0:T(4,128)}, u32[]{:S(2)}) %copy-start.2) | copy-done | bytes 72
  3.2 0.0 copy-start.3
  3.2 0.7 %copy-done.3 = s32[3,4]{1,0:T(4,128)S(1)} copy-done((s32[3,4]{1,0:T(4,128)S(1)}, s32[3,4]{1,0:T(4,128)}, u32[]{:S(2)}) %copy-start.3) | copy-done | bytes 72
  3.9 35.2 %shard_map.55 = bf16[3,4,64,128]{3,2,1,0:T(8,128)(2,1)S(1)} custom-call(s32[3,4]{1,0:T(4,128)S(1)} %copy-done.2, s32[3,4]{1,0:T(4,128)S(1)} %copy-done.3, s32[24]{0:T(128)S(1)} %copy-done.4, bf16[3,4,64,64]{3,2,1,0:T(8,128)(2,1)S(1)} %copy-done.1, bf16[3,4,64,128]{3,2,1,0:T(8,128)(2,1)S(1)} %copy-done, bf16[12,64,128]{2,1,0:T(8,128)(2,1)S(1)} %bitcast.1), custom_call_target="tpu_custom_call" | custom-call | tf_op jit(solution)/shard_map/pallas_call | solution.py:223
  39.1 0.7 %copy.7 = bf16[3,4,64,128]{3,2,1,0:T(8,128)(2,1)} copy(bf16[3,4,64,128]{3,2,1,0:T(8,128)(2,1)S(1)} %shard_map.55) | data formatting | bytes 393216
Async XLA Ops:
  0.0 0.7 %copy-start.4 = (s32[24]{0:T(128)S(1)}, s32[24]{0:T(128)}, u32[]{:S(2)}) copy-start(s32[24]{0:T(128)} %order_ref.1) | copy-start | bytes 292
  0.7 0.9 %copy-start = (bf16[3,4,64,128]{3,2,1,0:T(8,128)(2,1)S(1)}, bf16[3,4,64,128]{3,2,1,0:T(8,128)(2,1)}, u32[]{:S(2)}) copy-start(bf16[3,4,64,128]{3,2,1,0:T(8,128)(2,1)} %p_ref.1) | copy-start | bytes 589828
  1.6 0.9 %copy-start.1 = (bf16[3,4,64,64]{3,2,1,0:T(8,128)(2,1)S(1)}, bf16[3,4,64,64]{3,2,1,0:T(8,128)(2,1)}, u32[]{:S(2)}) copy-start(bf16[3,4,64,64]{3,2,1,0:T(8,128)(2,1)} %k_ref.1) | copy-start | bytes 294916
  2.5 0.7 %copy-start.2 = (s32[3,4]{1,0:T(4,128)S(1)}, s32[3,4]{1,0:T(4,128)}, u32[]{:S(2)}) copy-start(s32[3,4]{1,0:T(4,128)} %kc_ref.1) | copy-start | bytes 148
  3.2 0.7 %copy-start.3 = (s32[3,4]{1,0:T(4,128)S(1)}, s32[3,4]{1,0:T(4,128)}, u32[]{:S(2)}) copy-start(s32[3,4]{1,0:T(4,128)} %pc_ref.1) | copy-start | bytes 148

commit v2 on v1

--- a/solution.py
+++ b/solution.py
@@ -19,9 +19,10 @@
 
 def kernel(
     nrow, ncol, R, S, G,
-    kc_ref, pc_ref, order_ref, k_ref, p_ref, p_any, out_ref,
+    kc_ref, pc_ref, order_ref, k_ref, p_ref, out_ref,
     pbuf, kbuf, kcol, plcol, mrow, mcol, mrow_s, mcol_s, jout, accl, accr,
-    bar_unused, s_rp, r_rp, s_rk, r_rk, s_rm, r_rm, s_ck, r_ck, s_cp, r_cp, s_cm, r_cm, lsem,
+    kc, pc, order, kv,
+    s_rp, r_rp, s_rk, r_rk, s_rm, r_rm, s_fp, s_fk, s_ck, r_ck, s_cp, r_cp, s_cm, r_cm, lsem,
 ):
     r = lax.axis_index("row")
     c = lax.axis_index("col")
@@ -31,10 +32,15 @@
     SW = nrow * KB
     zero_p = nrow * PB
     zero_k = 2 * SW
-    B = k_ref.shape[2]
+    B = kv.shape[2]
+    relay = ncol == 4
 
     rows = [lax.rem(r + d, nrow) for d in range(1, nrow)]
     cols = [lax.rem(c + d, ncol) for d in range(1, ncol)]
+    core = lax.rem(r, 2)
+    sibling = r + 1 - 2 * core
+    same = [lax.rem(r + 2 * d, nrow) for d in range(1, nrow // 2)]
+    other = [lax.rem(sibling + 2 * d, nrow) for d in range(1, nrow // 2)]
 
     barrier = pltpu.get_barrier_semaphore()
     for peer in rows:
@@ -42,15 +48,25 @@
     for peer in cols:
         pl.semaphore_signal(barrier, inc=1, device_id={"col": peer}, device_id_type=MESH)
 
+    loads = [
+        pltpu.make_async_copy(src, dst, lsem.at[n])
+        for n, (src, dst) in enumerate((
+            (kc_ref, kc), (pc_ref, pc), (order_ref, order), (k_ref, kv),
+            (p_ref, pbuf.at[pl.ds(r * PB, PB)])))
+    ]
+    for cp in loads:
+        cp.start()
+    for cp in loads[:3]:
+        cp.wait()
+
     lane = lax.broadcasted_iota(jnp.int32, (1, LANES), 1)
     meta = jnp.zeros((1, LANES), jnp.int32)
-    entries = []
-    orders = [order_ref[c * G + j] for j in range(G)]
+    orders = [order[c * G + j] for j in range(G)]
     krow, kcl, prow, pcl = [], [], [], []
     t_p, t_kl, t_kh = [], [], []
     for i in range(R):
-        kcs = [kc_ref[i, s] for s in range(S)]
-        pcs = [pc_ref[i, s] for s in range(S)]
+        kcs = [kc[i, s] for s in range(S)]
+        pcs = [pc[i, s] for s in range(S)]
         khit = [[kcs[s] == orders[j] for j in range(G)] for s in range(S)]
         phit = [[pcs[s] == orders[j] for j in range(G)] for s in range(S)]
         for s in range(S):
@@ -86,81 +102,108 @@
     O_KC, O_PR, O_PC = O_KR + PB, O_KR + 2 * PB, O_KR + 3 * PB
     mrow[r] = meta
     mcol[c] = meta
-    empty = jnp.where(lane < O_KL, zero_p, zero_k)
-    mrow[nrow] = empty
-
+    mrow[nrow] = jnp.where(lane < O_KL, zero_p, zero_k)
+
+    for cp in loads[3:]:
+        cp.wait()
     low = lax.broadcasted_iota(jnp.int32, (B, 2 * B), 1) < B
     for i in range(R):
         for h in range(H):
-            pair = jnp.concatenate([k_ref[i, 2 * h], k_ref[i, 2 * h + 1]], axis=-1)
+            pair = jnp.concatenate([kv[i, 2 * h], kv[i, 2 * h + 1]], axis=-1)
             kbuf[r * KB + i * H + h] = pair
             kcol[c, i * H + h] = pair
-            a, b = p_ref[i, 2 * h], p_ref[i, 2 * h + 1]
+            a, b = pbuf[r * PB + i * S + 2 * h], pbuf[r * PB + i * S + 2 * h + 1]
             plcol[c, i * H + h, :B] = jnp.where(low, a, swap_halves(b))
             plcol[c, i * H + h, B:] = jnp.where(low, swap_halves(a), b)
 
     pl.semaphore_wait(barrier, nrow + ncol - 2)
 
-    def row_copies(src, d, peer):
-        return (
-            pltpu.make_async_remote_copy(
-                mrow.at[src], mrow.at[src], s_rm.at[d], r_rm.at[src],
-                device_id={"row": peer}, device_id_type=MESH),
-            pltpu.make_async_remote_copy(
-                kbuf.at[pl.ds(src * KB, KB)], kbuf.at[pl.ds(src * KB, KB)], s_rk.at[d], r_rk.at[src],
-                device_id={"row": peer}, device_id_type=MESH),
-            pltpu.make_async_remote_copy(
-                p_any, pbuf.at[pl.ds(src * PB, PB)], s_rp.at[d], r_rp.at[src],
-                device_id={"row": peer}, device_id_type=MESH),
-        )
-
-    def col_copies(src, d, peer):
-        return (
-            pltpu.make_async_remote_copy(
-                mcol.at[src], mcol.at[src], s_cm.at[d], r_cm.at[src],
-                device_id={"col": peer}, device_id_type=MESH),
-            pltpu.make_async_remote_copy(
-                kcol.at[src], kcol.at[src], s_ck.at[d], r_ck.at[src],
-                device_id={"col": peer}, device_id_type=MESH),
-            pltpu.make_async_remote_copy(
-                plcol.at[src], plcol.at[src], s_cp.at[d], r_cp.at[src],
-                device_id={"col": peer}, device_id_type=MESH),
-        )
-
-    sent = [row_copies(r, d, peer) for d, peer in enumerate(rows)]
-    sent_col = [col_copies(c, d, peer) for d, peer in enumerate(cols)]
-    for kind in range(3):
-        for cp in sent_col:
-            cp[kind].start()
-        for cp in sent:
-            cp[kind].start()
-
-    for i in range(R):
-        for s in range(S):
-            pbuf[r * PB + i * S + s] = p_ref[i, s]
+    def row_copy(kind, src, send, peer):
+        ref, recv = (
+            (mrow.at[src], r_rm), (kbuf.at[pl.ds(src * KB, KB)], r_rk), (pbuf.at[pl.ds(src * PB, PB)], r_rp)
+        )[kind]
+        return pltpu.make_async_remote_copy(
+            ref, ref, send, recv.at[src], device_id={"row": peer}, device_id_type=MESH)
+
+    def col_copy(kind, src, send, peer):
+        ref, recv = ((mcol, r_cm), (kcol, r_ck), (plcol, r_cp))[kind]
+        return pltpu.make_async_remote_copy(
+            ref.at[src], ref.at[src], send, recv.at[src], device_id={"col": peer}, device_id_type=MESH)
+
+    def row_got(kind, src):
+        row_copy(kind, src, s_rm.at[0], src).wait_recv()
+
+    def col_got(kind, src):
+        col_copy(kind, src, s_cm.at[0], src).wait_recv()
+
+    sent = []
+
+    def start(cp):
+        cp.start()
+        sent.append(cp)
+
+    for d, peer in enumerate(cols):
+        start(col_copy(0, c, s_cm.at[d], peer))
+    for d, peer in enumerate(rows):
+        start(row_copy(0, r, s_rm.at[d], peer))
+    if relay:
+        inner = (c == 1) | (c == 2)
+        mirror = jnp.where(c < 2, 1, -1)
+        plan = [c + 2 * mirror, c + mirror]
+        for d, peer in enumerate(plan):
+            for kind in (1, 2):
+                start(col_copy(kind, c, (s_ck, s_cp)[kind - 1].at[d], peer))
+
+        @pl.when(inner)
+        def _():
+            for kind in (1, 2):
+                col_copy(kind, c, (s_ck, s_cp)[kind - 1].at[2], c - mirror).start()
+    else:
+        for d, peer in enumerate(cols):
+            for kind in (1, 2):
+                start(col_copy(kind, c, (s_ck, s_cp)[kind - 1].at[d], peer))
+    for kind in (1, 2):
+        for d, peer in enumerate(same + [sibling]):
+            start(row_copy(kind, r, (s_rk, s_rp)[kind - 1].at[d], peer))
+
     zero = jnp.zeros((B, 2 * B), jnp.bfloat16)
     pbuf[zero_p] = zero
     kbuf[zero_k] = zero
-    for n in range(KB):
-        kbuf[SW + r * KB + n] = swap_halves(kbuf[r * KB + n])
-
-    for d, src in enumerate(rows):
-        row_copies(src, d, src)[0].wait_recv()
-    for d, src in enumerate(cols):
-        col_copies(src, d, src)[0].wait_recv()
-    one = pltpu.make_async_copy(mrow, mrow_s, lsem.at[0])
-    two = pltpu.make_async_copy(mcol, mcol_s, lsem.at[1])
-    one.start()
-    two.start()
-    one.wait()
-    two.wait()
-
-    for d, src in enumerate(rows):
-        row_copies(src, d, src)[1].wait_recv()
+
+    def swapped(src):
         for n in range(KB):
             kbuf[SW + src * KB + n] = swap_halves(kbuf[src * KB + n])
-    for d, src in enumerate(rows):
-        row_copies(src, d, src)[2].wait_recv()
+
+    swapped(r)
+
+    for src in rows:
+        row_got(0, src)
+    for src in cols:
+        col_got(0, src)
+    tables = [pltpu.make_async_copy(mrow, mrow_s, lsem.at[0]), pltpu.make_async_copy(mcol, mcol_s, lsem.at[1])]
+    for cp in tables:
+        cp.start()
+    for cp in tables:
+        cp.wait()
+
+    for d, src in enumerate(same):
+        row_got(1, src)
+        start(row_copy(1, src, s_fk.at[d], sibling))
+        swapped(src)
+    if relay:
+        @pl.when(inner)
+        def _():
+            for kind in (1, 2):
+                col_got(kind, jnp.where(c == 1, 3, 0))
+                col_copy(kind, jnp.where(c == 1, 3, 0), (s_ck, s_cp)[kind - 1].at[3], c - mirror).start()
+    for d, src in enumerate(same):
+        row_got(2, src)
+        start(row_copy(2, src, s_fp.at[d], sibling))
+    for src in [sibling] + other:
+        row_got(1, src)
+        swapped(src)
+    for src in [sibling] + other:
+        row_got(2, src)
 
     def add(g, first):
         for i in range(R):
@@ -190,9 +233,18 @@
     add(c, True)
 
     def step(d, carry):
-        src = lax.rem(c + d, ncol)
-        for cp in col_copies(src, 0, src)[1:]:
-            cp.wait_recv()
+        if relay:
+            src = lax.rem(c + mirror * d + ncol, ncol)
+            taken = inner & (src == jnp.where(c == 1, 3, 0))
+
+            @pl.when(jnp.logical_not(taken))
+            def _():
+                col_got(1, src)
+                col_got(2, src)
+        else:
+            src = lax.rem(c + d, ncol)
+            col_got(1, src)
+            col_got(2, src)
         add(src, False)
         return carry
 
@@ -207,9 +259,14 @@
             for t, pk in ((2 * h, first), (2 * h + 1, second)):
                 out_ref[i, t] = (accl[i, :, t * 2 * B:(t + 1) * 2 * B] - pk).astype(out_ref.dtype)
 
-    for cps in sent + sent_col:
-        for cp in cps:
-            cp.wait_send()
+    for cp in sent:
+        cp.wait_send()
+    if relay:
+        @pl.when(inner)
+        def _():
+            for kind in (1, 2):
+                for n in (2, 3):
+                    col_copy(kind, c, (s_ck, s_cp)[kind - 1].at[n], c - mirror).wait_send()
 
 
 def per_device(nrow, ncol, k_blocks, p_blocks, k_columns, p_columns, molecule_order):
@@ -218,12 +275,12 @@
     H = S // 2
     bf, i32 = jnp.bfloat16, jnp.int32
     vmem = pl.BlockSpec(memory_space=pltpu.VMEM)
-    smem = pl.BlockSpec(memory_space=pltpu.SMEM)
+    anywhere = pl.BlockSpec(memory_space=pl.ANY)
     dma = pltpu.SemaphoreType.DMA
     return pl.pallas_call(
         functools.partial(kernel, nrow, ncol, R, S, G),
         out_shape=jax.ShapeDtypeStruct(p_blocks.shape, bf),
-        in_specs=[smem, smem, smem, vmem, vmem, pl.BlockSpec(memory_space=pl.ANY)],
+        in_specs=[anywhere] * 5,
         out_specs=vmem,
         scratch_shapes=[
             pltpu.VMEM((nrow * R * S + 1, B, W), bf),
@@ -237,15 +294,18 @@
             pltpu.SMEM((R * S,), i32),
             pltpu.VMEM((R, B, S * W), jnp.float32),
             pltpu.VMEM((R, 2 * B, S * B), jnp.float32),
-            dma((1,)),
-            dma((nrow,)), dma((nrow,)), dma((nrow,)), dma((nrow,)), dma((nrow,)), dma((nrow,)),
-            dma((ncol,)), dma((ncol,)), dma((ncol,)), dma((ncol,)), dma((ncol,)), dma((ncol,)),
-            dma((2,)),
+            pltpu.SMEM((R, S), i32),
+            pltpu.SMEM((R, S), i32),
+            pltpu.SMEM(molecule_order.shape, i32),
+            pltpu.VMEM((R, S, B, B), bf),
+            *[dma((nrow,))] * 8,
+            *[dma((ncol,))] * 6,
+            dma((5,)),
         ],
         compiler_params=pltpu.CompilerParams(
             collective_id=0, has_side_effects=True, vmem_limit_bytes=48 << 20),
     )(k_columns, p_columns, molecule_order, k_blocks,
-      p_blocks, p_blocks.reshape(R * S, B, W))
+      p_blocks.reshape(R * S, B, W))
 
 
 def solution(mesh):

time: 39.9 us -> 31.7 us (0.79)
  the two profiles are of different devices: /device:TPU:1 before, /device:TPU:0 now
where the time goes in v2:
time: 31.7 us; the launch traced here: 31.5 us
  Pallas kernels  27 us (85%)
  local copies, waits for them, and re-layouts  4.55 us (14%)
    pallas_call x1, Pallas kernels, per_device(): pl.pallas_call(functools.partial(kernel, nrow, ncol, R, S, G), out_shape=...  27 us
    unnamed x11, local copies, waits for them, and re-layouts  4.55 us

profile of v2, /device:TPU:0, one launch (start us, length us, event | category | flops | bytes accessed | tf_op | source)
XLA Modules:
  0.0 31.5 jit_solution(6114135794758417902)
XLA Ops:
  0.0 0.0 copy-start.4
  0.0 0.7 %copy-done.4 = s32[24]{0:T(128)S(1)} copy-done((s32[24]{0:T(128)S(1)}, s32[24]{0:T(128)}, u32[]{:S(2)}) %copy-start.4) | copy-done | bytes 120
  0.7 0.0 copy-start
  0.7 0.9 %copy-done = bf16[3,4,64,64]{3,2,1,0:T(8,128)(2,1)S(1)} copy-done((bf16[3,4,64,64]{3,2,1,0:T(8,128)(2,1)S(1)}, bf16[3,4,64,64]{3,2,1,0:T(8,128)(2,1)}, u32[]{:S(2)}) %copy-start) | copy-done | bytes 98328
  1.6 0.0 copy-start.1
  1.6 0.9 %copy-done.1 = bf16[3,4,64,128]{3,2,1,0:T(8,128)(2,1)S(1)} copy-done((bf16[3,4,64,128]{3,2,1,0:T(8,128)(2,1)S(1)}, bf16[3,4,64,128]{3,2,1,0:T(8,128)(2,1)}, u32[]{:S(2)}) %copy-start.1) | copy-done | bytes 196632
  2.5 0.0 copy-start.2
  2.5 0.7 %copy-done.2 = s32[3,4]{1,0:T(4,128)S(1)} copy-done((s32[3,4]{1,0:T(4,128)S(1)}, s32[3,4]{1,0:T(4,128)}, u32[]{:S(2)}) %copy-start.2) | copy-done | bytes 72
  3.2 0.0 copy-start.3
  3.2 0.7 %copy-done.3 = s32[3,4]{1,0:T(4,128)S(1)} copy-done((s32[3,4]{1,0:T(4,128)S(1)}, s32[3,4]{1,0:T(4,128)}, u32[]{:S(2)}) %copy-start.3) | copy-done | bytes 72
  3.9 27.0 %shard_map.55 = bf16[3,4,64,128]{3,2,1,0:T(8,128)(2,1)S(1)} custom-call(s32[3,4]{1,0:T(4,128)S(1)} %copy-done.2, s32[3,4]{1,0:T(4,128)S(1)} %copy-done.3, s32[24]{0:T(128)S(1)} %copy-done.4, bf16[3,4,64,64]{3,2,1,0:T(8,128)(2,1)S(1)} %copy-done, bf16[12,64,128]{2,1,0:T(8,128)(2,1)S(1)} %bitcast.1), custom_call_target="tpu_custom_call" | custom-call | tf_op jit(solution)/shard_map/pallas_call | solution.py:280
  30.8 0.7 %copy.7 = bf16[3,4,64,128]{3,2,1,0:T(8,128)(2,1)} copy(bf16[3,4,64,128]{3,2,1,0:T(8,128)(2,1)S(1)} %shard_map.55) | data formatting | bytes 393216
Async XLA Ops:
  0.0 0.7 %copy-start.4 = (s32[24]{0:T(128)S(1)}, s32[24]{0:T(128)}, u32[]{:S(2)}) copy-start(s32[24]{0:T(128)} %order_ref.1) | copy-start | bytes 292
  0.7 0.9 %copy-start = (bf16[3,4,64,64]{3,2,1,0:T(8,128)(2,1)S(1)}, bf16[3,4,64,64]{3,2,1,0:T(8,128)(2,1)}, u32[]{:S(2)}) copy-start(bf16[3,4,64,64]{3,2,1,0:T(8,128)(2,1)} %k_ref.1) | copy-start | bytes 294916
  1.6 0.9 %copy-start.1 = (bf16[3,4,64,128]{3,2,1,0:T(8,128)(2,1)S(1)}, bf16[3,4,64,128]{3,2,1,0:T(8,128)(2,1)}, u32[]{:S(2)}) copy-start(bf16[3,4,64,128]{3,2,1,0:T(8,128)(2,1)} %param.6) | copy-start | bytes 589828
  2.5 0.7 %copy-start.2 = (s32[3,4]{1,0:T(4,128)S(1)}, s32[3,4]{1,0:T(4,128)}, u32[]{:S(2)}) copy-start(s32[3,4]{1,0:T(4,128)} %kc_ref.1) | copy-start | bytes 148
  3.2 0.7 %copy-start.3 = (s32[3,4]{1,0:T(4,128)S(1)}, s32[3,4]{1,0:T(4,128)}, u32[]{:S(2)}) copy-start(s32[3,4]{1,0:T(4,128)} %pc_ref.1) | copy-start | bytes 148

commit v3 on v2

--- a/solution.py
+++ b/solution.py
@@ -56,6 +56,7 @@
     ]
     for cp in loads:
         cp.start()
+
     for cp in loads[:3]:
         cp.wait()
 
@@ -176,6 +177,25 @@
 
     swapped(r)
 
+    if relay:
+        @pl.when(inner)
+        def _():
+            for kind in (1, 2):
+                col_got(kind, jnp.where(c == 1, 3, 0))
+                col_copy(kind, jnp.where(c == 1, 3, 0), (s_ck, s_cp)[kind - 1].at[3], c - mirror).start()
+    for d, src in enumerate(same):
+        row_got(1, src)
+        start(row_copy(1, src, s_fk.at[d], sibling))
+        swapped(src)
+    for d, src in enumerate(same):
+        row_got(2, src)
+        start(row_copy(2, src, s_fp.at[d], sibling))
+    for src in [sibling] + other:
+        row_got(1, src)
+        swapped(src)
+    for src in [sibling] + other:
+        row_got(2, src)
+
     for src in rows:
         row_got(0, src)
     for src in cols:
@@ -185,25 +205,6 @@
         cp.start()
     for cp in tables:
         cp.wait()
-
-    for d, src in enumerate(same):
-        row_got(1, src)
-        start(row_copy(1, src, s_fk.at[d], sibling))
-        swapped(src)
-    if relay:
-        @pl.when(inner)
-        def _():
-            for kind in (1, 2):
-                col_got(kind, jnp.where(c == 1, 3, 0))
-                col_copy(kind, jnp.where(c == 1, 3, 0), (s_ck, s_cp)[kind - 1].at[3], c - mirror).start()
-    for d, src in enumerate(same):
-        row_got(2, src)
-        start(row_copy(2, src, s_fp.at[d], sibling))
-    for src in [sibling] + other:
-        row_got(1, src)
-        swapped(src)
-    for src in [sibling] + other:
-        row_got(2, src)
 
     def add(g, first):
         for i in range(R):
@@ -275,7 +276,7 @@
     H = S // 2
     bf, i32 = jnp.bfloat16, jnp.int32
     vmem = pl.BlockSpec(memory_space=pltpu.VMEM)
-    anywhere = pl.BlockSpec(memory_space=pl.ANY)
+    anywhere = pl.BlockSpec(memory_space=pltpu.HBM)
     dma = pltpu.SemaphoreType.DMA
     return pl.pallas_call(
         functools.partial(kernel, nrow, ncol, R, S, G),
@@ -303,7 +304,7 @@
             dma((5,)),
         ],
         compiler_params=pltpu.CompilerParams(
-            collective_id=0, has_side_effects=True, vmem_limit_bytes=48 << 20),
+            collective_id=0, has_side_effects=True, vmem_limit_bytes=60 << 20),
     )(k_columns, p_columns, molecule_order, k_blocks,
       p_blocks.reshape(R * S, B, W))
 

time: 31.7 us -> 29.4 us (0.927)
  local copies, waits for them, and re-layouts: 4.55 us -> 1.62 us
  Pallas kernels: 27 us -> 27.6 us
    unnamed x11 -> x1, local copies, waits for them, and re-layouts: 4.55 us -> 1.62 us
    pallas_call x1, Pallas kernels: 27 us -> 27.6 us  [per_device(): pl.pallas_call(functools.partial(kernel, nrow, ncol, R, S, G), out_shape=...]
where the time goes in v3:
time: 29.4 us; the launch traced here: 29.2 us
  Pallas kernels  27.6 us (94%)
  local copies, waits for them, and re-layouts  1.62 us (6%)
    pallas_call x1, Pallas kernels, per_device(): pl.pallas_call(functools.partial(kernel, nrow, ncol, R, S, G), out_shape=...  27.6 us
    unnamed x1, local copies, waits for them, and re-layouts  1.62 us

profile of v3, /device:TPU:0, one launch (start us, length us, event | category | flops | bytes accessed | tf_op | source)
XLA Modules:
  0.0 29.2 jit_solution(17607658005438493901)
XLA Ops:
  0.0 27.6 %shard_map.55 = bf16[3,4,64,128]{3,2,1,0:T(8,128)(2,1)} custom-call(s32[3,4]{1,0:T(4,128)} %kc_ref.1, s32[3,4]{1,0:T(4,128)} %pc_ref.1, s32[24]{0:T(128)} %order_ref.1, bf16[3,4,64,64]{3,2,1,0:T(8,128)(2,1)} %k_ref.1, bf16[12,64,128]{2,1,0:T(8,128)(2,1)} %bitcast.1), custom_call_target="tpu_custom_call" | custom-call | tf_op jit(solution)/shard_map/pallas_call | solution.py:281
  27.6 1.6 %copy.7 = bf16[3,4,64,128]{3,2,1,0:T(8,128)(2,1)} copy(bf16[3,4,64,128]{3,2,1,0:T(8,128)(2,1)} %shard_map.55) | data formatting | bytes 393216

commit v4 on v3

--- a/solution.py
+++ b/solution.py
@@ -22,7 +22,7 @@
     kc_ref, pc_ref, order_ref, k_ref, p_ref, out_ref,
     pbuf, kbuf, kcol, plcol, mrow, mcol, mrow_s, mcol_s, jout, accl, accr,
     kc, pc, order, kv,
-    s_rp, r_rp, s_rk, r_rk, s_rm, r_rm, s_fp, s_fk, s_ck, r_ck, s_cp, r_cp, s_cm, r_cm, lsem,
+    s_rp, r_rp, s_rk, r_rk, s_rm, r_rm, s_fm, s_fp, s_fk, s_ck, r_ck, s_cp, r_cp, s_cm, r_cm, lsem,
 ):
     r = lax.axis_index("row")
     c = lax.axis_index("col")
@@ -43,10 +43,24 @@
     other = [lax.rem(sibling + 2 * d, nrow) for d in range(1, nrow // 2)]
 
     barrier = pltpu.get_barrier_semaphore()
-    for peer in rows:
+    near = same + [sibling] if relay else rows
+    for peer in near:
         pl.semaphore_signal(barrier, inc=1, device_id={"row": peer}, device_id_type=MESH)
-    for peer in cols:
-        pl.semaphore_signal(barrier, inc=1, device_id={"col": peer}, device_id_type=MESH)
+    if relay:
+        inner = (c == 1) | (c == 2)
+        mirror = jnp.where(c < 2, 1, -1)
+        far = jnp.where(c == 1, 3, 0)
+        has = (c < ncol - 1, c > 0)
+        step_to = (c + 1, c - 1)
+        arrivals = len(near) + jnp.where(inner, 2, 1)
+        for ok, peer in zip(has, step_to):
+            @pl.when(ok)
+            def _(peer=peer):
+                pl.semaphore_signal(barrier, inc=1, device_id={"col": peer}, device_id_type=MESH)
+    else:
+        arrivals = nrow + ncol - 2
+        for peer in cols:
+            pl.semaphore_signal(barrier, inc=1, device_id={"col": peer}, device_id_type=MESH)
 
     loads = [
         pltpu.make_async_copy(src, dst, lsem.at[n])
@@ -117,7 +131,7 @@
             plcol[c, i * H + h, :B] = jnp.where(low, a, swap_halves(b))
             plcol[c, i * H + h, B:] = jnp.where(low, swap_halves(a), b)
 
-    pl.semaphore_wait(barrier, nrow + ncol - 2)
+    pl.semaphore_wait(barrier, arrivals)
 
     def row_copy(kind, src, send, peer):
         ref, recv = (
@@ -143,29 +157,25 @@
         cp.start()
         sent.append(cp)
 
-    for d, peer in enumerate(cols):
-        start(col_copy(0, c, s_cm.at[d], peer))
-    for d, peer in enumerate(rows):
-        start(row_copy(0, r, s_rm.at[d], peer))
-    if relay:
-        inner = (c == 1) | (c == 2)
-        mirror = jnp.where(c < 2, 1, -1)
-        plan = [c + 2 * mirror, c + mirror]
-        for d, peer in enumerate(plan):
-            for kind in (1, 2):
-                start(col_copy(kind, c, (s_ck, s_cp)[kind - 1].at[d], peer))
-
-        @pl.when(inner)
-        def _():
-            for kind in (1, 2):
-                col_copy(kind, c, (s_ck, s_cp)[kind - 1].at[2], c - mirror).start()
+    col_sems = (s_cm, s_ck, s_cp)
+
+    def pass_on(kind, src, slot, peer):
+        return col_copy(kind, src, col_sems[kind].at[slot], peer)
+
+    if relay:
+        for kind in range(3):
+            for n, (ok, peer) in enumerate(zip(has, step_to)):
+                @pl.when(ok)
+                def _(kind=kind, n=n, peer=peer):
+                    pass_on(kind, c, n, peer).start()
+            for d, peer in enumerate(near):
+                start(row_copy(kind, r, (s_rm, s_rk, s_rp)[kind].at[d], peer))
     else:
-        for d, peer in enumerate(cols):
-            for kind in (1, 2):
-                start(col_copy(kind, c, (s_ck, s_cp)[kind - 1].at[d], peer))
-    for kind in (1, 2):
-        for d, peer in enumerate(same + [sibling]):
-            start(row_copy(kind, r, (s_rk, s_rp)[kind - 1].at[d], peer))
+        for kind in range(3):
+            for d, peer in enumerate(cols):
+                start(pass_on(kind, c, d, peer))
+            for d, peer in enumerate(same + [sibling] if kind else rows):
+                start(row_copy(kind, r, (s_rm, s_rk, s_rp)[kind].at[d], peer))
 
     zero = jnp.zeros((B, 2 * B), jnp.bfloat16)
     pbuf[zero_p] = zero
@@ -177,29 +187,51 @@
 
     swapped(r)
 
-    if relay:
-        @pl.when(inner)
-        def _():
-            for kind in (1, 2):
-                col_got(kind, jnp.where(c == 1, 3, 0))
-                col_copy(kind, jnp.where(c == 1, 3, 0), (s_ck, s_cp)[kind - 1].at[3], c - mirror).start()
+    def inside(kinds, hops):
+        if relay:
+            @pl.when(inner)
+            def _():
+                for kind in kinds:
+                    for src, slot, peer in hops:
+                        col_got(kind, src)
+                        pass_on(kind, src, slot, peer).start()
+
+    if relay:
+        onward = [(c - 1, 2, c + 1), (c + 1, 3, c - 1)]
+        last = [(far, 4, c - mirror)]
+    else:
+        onward = last = []
+    inside((0, 1), onward)
     for d, src in enumerate(same):
+        if relay:
+            row_got(0, src)
+            start(row_copy(0, src, s_fm.at[d], sibling))
         row_got(1, src)
         start(row_copy(1, src, s_fk.at[d], sibling))
+    inside((2,), onward)
+    for src in same:
         swapped(src)
+    inside((0, 1), last)
     for d, src in enumerate(same):
         row_got(2, src)
         start(row_copy(2, src, s_fp.at[d], sibling))
+    inside((2,), last)
     for src in [sibling] + other:
         row_got(1, src)
         swapped(src)
     for src in [sibling] + other:
         row_got(2, src)
 
-    for src in rows:
+    for src in [sibling] + other if relay else rows:
         row_got(0, src)
-    for src in cols:
-        col_got(0, src)
+    if relay:
+        @pl.when(jnp.logical_not(inner))
+        def _():
+            for d in range(1, ncol):
+                col_got(0, c + mirror * d)
+    else:
+        for src in cols:
+            col_got(0, src)
     tables = [pltpu.make_async_copy(mrow, mrow_s, lsem.at[0]), pltpu.make_async_copy(mcol, mcol_s, lsem.at[1])]
     for cp in tables:
         cp.start()
@@ -236,9 +268,7 @@
     def step(d, carry):
         if relay:
             src = lax.rem(c + mirror * d + ncol, ncol)
-            taken = inner & (src == jnp.where(c == 1, 3, 0))
-
-            @pl.when(jnp.logical_not(taken))
+            @pl.when(jnp.logical_not(inner))
             def _():
                 col_got(1, src)
                 col_got(2, src)
@@ -263,11 +293,17 @@
     for cp in sent:
         cp.wait_send()
     if relay:
+        for n, (ok, peer) in enumerate(zip(has, step_to)):
+            @pl.when(ok)
+            def _(n=n, peer=peer):
+                for kind in range(3):
+                    pass_on(kind, c, n, peer).wait_send()
+
         @pl.when(inner)
         def _():
-            for kind in (1, 2):
-                for n in (2, 3):
-                    col_copy(kind, c, (s_ck, s_cp)[kind - 1].at[n], c - mirror).wait_send()
+            for kind in range(3):
+                for src, slot, peer in onward + last:
+                    pass_on(kind, src, slot, peer).wait_send()
 
 
 def per_device(nrow, ncol, k_blocks, p_blocks, k_columns, p_columns, molecule_order):
@@ -299,8 +335,8 @@
             pltpu.SMEM((R, S), i32),
             pltpu.SMEM(molecule_order.shape, i32),
             pltpu.VMEM((R, S, B, B), bf),
-            *[dma((nrow,))] * 8,
-            *[dma((ncol,))] * 6,
+            *[dma((nrow,))] * 9,
+            *[dma((ncol + 1,))] * 6,
             dma((5,)),
         ],
         compiler_params=pltpu.CompilerParams(

time: 29.4 us -> 28.9 us (0.983)
  Pallas kernels: 27.6 us -> 27.2 us
    pallas_call x1, Pallas kernels: 27.6 us -> 27.2 us  [per_device(): pl.pallas_call(functools.partial(kernel, nrow, ncol, R, S, G), out_shape=...]
where the time goes in v4:
time: 28.9 us; the launch traced here: 28.8 us
  Pallas kernels  27.2 us (94%)
  local copies, waits for them, and re-layouts  1.62 us (6%)
    pallas_call x1, Pallas kernels, per_device(): pl.pallas_call(functools.partial(kernel, nrow, ncol, R, S, G), out_shape=...  27.2 us
    unnamed x1, local copies, waits for them, and re-layouts  1.62 us

profile of v4, /device:TPU:0, one launch (start us, length us, event | category | flops | bytes accessed | tf_op | source)
XLA Modules:
  0.0 28.8 jit_solution(5152216940241484463)
XLA Ops:
  0.0 27.2 %shard_map.55 = bf16[3,4,64,128]{3,2,1,0:T(8,128)(2,1)} custom-call(s32[3,4]{1,0:T(4,128)} %kc_ref.1, s32[3,4]{1,0:T(4,128)} %pc_ref.1, s32[24]{0:T(128)} %order_ref.1, bf16[3,4,64,64]{3,2,1,0:T(8,128)(2,1)} %k_ref.1, bf16[12,64,128]{2,1,0:T(8,128)(2,1)} %bitcast.1), custom_call_target="tpu_custom_call" | custom-call | tf_op jit(solution)/shard_map/pallas_call | solution.py:317
  27.2 1.6 %copy.7 = bf16[3,4,64,128]{3,2,1,0:T(8,128)(2,1)} copy(bf16[3,4,64,128]{3,2,1,0:T(8,128)(2,1)} %shard_map.55) | data formatting | bytes 393216

commit v5 on v4

--- a/solution.py
+++ b/solution.py
@@ -168,6 +168,7 @@
                 @pl.when(ok)
                 def _(kind=kind, n=n, peer=peer):
                     pass_on(kind, c, n, peer).start()
+        for kind in range(3):
             for d, peer in enumerate(near):
                 start(row_copy(kind, r, (s_rm, s_rk, s_rp)[kind].at[d], peer))
     else:

time: 28.9 us -> 28.9 us (level)
  no operation moved by 1% of the time
where the time goes in v5:
time: 28.9 us; the launch traced here: 28.8 us
  Pallas kernels  27.2 us (94%)
  local copies, waits for them, and re-layouts  1.62 us (6%)
    pallas_call x1, Pallas kernels, per_device(): pl.pallas_call(functools.partial(kernel, nrow, ncol, R, S, G), out_shape=...  27.2 us
    unnamed x1, local copies, waits for them, and re-layouts  1.62 us

profile of v5, /device:TPU:0, one launch (start us, length us, event | category | flops | bytes accessed | tf_op | source)
XLA Modules:
  0.0 28.8 jit_solution(2724000976667400531)
XLA Ops:
  0.0 27.2 %shard_map.55 = bf16[3,4,64,128]{3,2,1,0:T(8,128)(2,1)} custom-call(s32[3,4]{1,0:T(4,128)} %kc_ref.1, s32[3,4]{1,0:T(4,128)} %pc_ref.1, s32[24]{0:T(128)} %order_ref.1, bf16[3,4,64,64]{3,2,1,0:T(8,128)(2,1)} %k_ref.1, bf16[12,64,128]{2,1,0:T(8,128)(2,1)} %bitcast.1), custom_call_target="tpu_custom_call" | custom-call | tf_op jit(solution)/shard_map/pallas_call | solution.py:318
  27.2 1.6 %copy.7 = bf16[3,4,64,128]{3,2,1,0:T(8,128)(2,1)} copy(bf16[3,4,64,128]{3,2,1,0:T(8,128)(2,1)} %shard_map.55) | data formatting | bytes 393216
